TPU v7x, 32 devices: a whole 2x2x4 slice. The times are simulated.
32 devices in a mesh: pair: 2 (over core), vcol: 16 (over z, y, x).
Axes of the slice: x: 2, y: 2, z: 4, core: 2. Of those that a mesh axis runs over, the one named last changes fastest.
Arguments:
- amplitudes: bfloat16 [1280, 4096], P('pair', 'vcol'), may hold values from -6 to 6
- tile_owner: int32 [32], replicated, may hold values from 0 to 31, each once
- integrals: bfloat16 [4096, 4096], P('pair', 'vcol'), may hold values from -0.125 to 0.125
- screening: int32 [20, 32, 32], P('pair'), may hold values 0 or 1
- occ_energy: float32 [1280], P('pair'), may hold values from -1 to -0.2
- virt_energy: float32 [4096], replicated, may hold values from 0.2 to 1
Outputs:
- residual: bfloat16 [1280, 4096], P('pair', 'vcol')
Inputs may be any that keep to these rules, and one draw needn't show every extreme that they name: `tile_owner`: each of the 32 tiles appears exactly once.
All inputs are finite; a program needn't handle non-finite values. No bound on the sum of `screening` on one device may be relied on, other than what follows from the above.
Results may differ from a plain program's by a relative error of at most 0.0036.
Values may be sent and summed in bfloat16 or wider, within the bound.
A program may use at most 64 MiB of HBM per device.

v0:
```python
import functools

import jax
import jax.numpy as jnp
from jax import lax
from jax.experimental import pallas as pl
from jax.experimental.pallas import tpu as pltpu
from jax.sharding import PartitionSpec as P

TILE = 128
PBLK = 64
KT_DEV = 2
MESH = pl.DeviceIdType.MESH


def one_hot(indices, length):
    return (indices[:, None] == jnp.arange(length, dtype=jnp.int32)[None, :]).astype(jnp.float32)


def ladder_kernel(
    ranks, pairs, owner, screen, amps, ints, out,
    gath, panel, lhs, acc, parts, natural, slots, landed,
    local_sem, send_sem, recv_sem, pair_send, pair_recv, out_send, out_recv, back_send, back_recv,
):
    length = ranks // 4
    me = lax.axis_index("vcol")
    core = lax.axis_index("pair")
    line, spot = me // 4, me % 4
    hi, lo = spot // 2, spot % 2
    turn = core % 2
    flip_lo, flip_hi = hi * 2 + 1 - lo, (1 - hi) * 2 + lo
    first = (1 - turn) * flip_lo + turn * flip_hi
    second = turn * flip_lo + (1 - turn) * flip_hi
    across = 3 - spot
    rows = gath.shape[1]
    blocks = rows // PBLK
    tiles = ints.shape[0]

    own_amps = pltpu.make_async_copy(amps, gath.at[me], local_sem.at[0])
    own_ints = pltpu.make_async_copy(ints, panel.at[pl.ds(core * tiles, tiles)], local_sem.at[1])
    own_amps.start()
    own_ints.start()

    has_up, has_down = line < length - 1, line > 0
    first_rank, second_rank = line * 4 + first, line * 4 + second
    barrier = pltpu.get_barrier_semaphore()

    def greet(target):
        pl.semaphore_signal(barrier, inc=1, device_id={"vcol": target}, device_id_type=MESH)

    def greet_step(step, _):
        greet((me + step) % ranks)
        return 0

    lax.fori_loop(1, ranks, greet_step, 0)
    for step in range(1, pairs):
        pl.semaphore_signal(
            barrier, inc=1, device_id={"pair": (core + step) % pairs}, device_id_type=MESH
        )

    pl.semaphore_wait(barrier, ranks - 1 + pairs - 1)

    cut = (blocks * 3 // 5) * PBLK
    bands = ((0, cut), (cut, rows))

    def shard(source, band, way, target):
        low, high = bands[band]
        place = gath.at[source, pl.ds(low, high - low)]
        return pltpu.make_async_remote_copy(
            src_ref=place, dst_ref=place,
            send_sem=send_sem.at[band, way, source], recv_sem=recv_sem.at[band, source],
            device_id={"vcol": target}, device_id_type=MESH,
        )

    def panel_copy(step):
        return pltpu.make_async_remote_copy(
            src_ref=ints, dst_ref=panel.at[pl.ds(core * tiles, tiles)],
            send_sem=pair_send.at[step - 1], recv_sem=pair_recv.at[step - 1],
            device_id={"pair": (core + step) % pairs}, device_id_type=MESH,
        )

    def arrived(source, band):
        shard(source, band, 3, second_rank).wait_recv()

    def multiply(source, band):
        low, high = bands[band]
        t0, t1 = owner[KT_DEV * source], owner[KT_DEV * source + 1]
        for slot, tile in enumerate((t0, t1)):
            columns = slice(slot * TILE, (slot + 1) * TILE)
            for block in range(low // PBLK, high // PBLK):
                part = slice(block * PBLK, (block + 1) * PBLK)
                value = gath[source, part, columns]
                for n in range(KT_DEV):
                    mark = screen[block, tile, KT_DEV * me + n].astype(jnp.float32)
                    lhs[n, part, columns] = value * jnp.full(value.shape, mark, jnp.float32).astype(
                        value.dtype
                    )
        right = jnp.concatenate([panel[t0], panel[t1]], axis=0)
        for n in range(KT_DEV):
            columns = slice(n * TILE, (n + 1) * TILE)
            acc[low:high, columns] += jnp.dot(
                lhs[n, low:high], right[:, columns], preferred_element_type=jnp.float32
            )

    def offset(e):
        return ((e + 1) // 2) * (1 - 2 * (e % 2))

    def inside(e):
        at = line + offset(e)
        return (at >= 0) & (at < length)

    own_amps.wait()

    def along_line(source, band, e, action):
        @pl.when(((e % 2 == 1) | (e == 0)) & has_up)
        def _():
            action(shard(source, band, 0, me + 4))

        @pl.when((e % 2 == 0) & has_down)
        def _():
            action(shard(source, band, 1, me - 4))

    def start(copy):
        copy.start()

    def wait_send(copy):
        copy.wait_send()

    def forward(source, band, e):
        along_line(source, band, e, start)
        shard(source, band, 2, first_rank).start()
        shard(source, band, 3, second_rank).start()

    for band in (1, 0):
        forward(me, band, jnp.int32(0))
    for step in range(1, pairs):
        panel_copy(step).start()
    acc[...] = jnp.zeros_like(acc)
    own_ints.wait()
    for step in range(1, pairs):
        panel_copy(step).wait_recv()
    for band in (1, 0):
        multiply(me, band)

    last = 2 * length - 1

    def on_column(e, _):
        source = (line + offset(e)) * 4 + spot

        @pl.when((e < last) & inside(e))
        def _():
            for band in (1, 0):
                arrived(source, band)
                forward(source, band, e)
            for band in (1, 0):
                multiply(source, band)

        late = e - 2
        beside = (line + offset(late)) * 4 + first

        @pl.when((late >= 0) & (late < last) & inside(late))
        def _():
            arrived(beside, 1)

            @pl.when(late == 0)
            def _():
                shard(beside, 1, 3, second_rank).start()

            arrived(beside, 0)
            shard(beside, 0, 3, second_rank).start()
            for band in (1, 0):
                multiply(beside, band)

        later = e - 4
        corner = (line + offset(later)) * 4 + across

        @pl.when((later >= 0) & inside(later))
        def _():
            arrived(corner, 1)
            along_line(corner, 1, later, start)
            multiply(corner, 1)

        return 0

    lax.fori_loop(1, last + 4, on_column, 0)

    def far_side(e, _):
        @pl.when((e < last) & inside(e))
        def _():
            source = (line + offset(e)) * 4 + second
            for band in (1, 0):
                arrived(source, band)
                multiply(source, band)

        late = e - 2

        @pl.when((late >= 0) & inside(late))
        def _():
            source = (line + offset(late)) * 4 + across
            arrived(source, 0)
            multiply(source, 0)

        return 0

    lax.fori_loop(0, last + 2, far_side, 0)

    part = rows // ranks
    for i in range(ranks):
        for n in range(KT_DEV):
            parts[i, n] = acc[i * part : (i + 1) * part, n * TILE : (n + 1) * TILE].astype(
                parts.dtype
            )

    def out_copy(step):
        target = (me + step) % ranks
        return pltpu.make_async_remote_copy(
            src_ref=parts.at[target], dst_ref=natural.at[pl.ds(KT_DEV * me, KT_DEV)],
            send_sem=out_send.at[step - 1], recv_sem=out_recv.at[step - 1],
            device_id={"vcol": target}, device_id_type=MESH,
        )

    def back_copy(step):
        target = (me + step) % ranks
        return pltpu.make_async_remote_copy(
            src_ref=slots.at[pl.ds(KT_DEV * target, KT_DEV)], dst_ref=landed.at[me],
            send_sem=back_send.at[step - 1], recv_sem=back_recv.at[step - 1],
            device_id={"vcol": target}, device_id_type=MESH,
        )

    def each_peer(action):
        def body(step, _):
            action(step)
            return 0

        lax.fori_loop(1, ranks, body, 0)

    own_out = pltpu.make_async_copy(
        parts.at[me], natural.at[pl.ds(KT_DEV * me, KT_DEV)], local_sem.at[2]
    )
    own_back = pltpu.make_async_copy(
        slots.at[pl.ds(KT_DEV * me, KT_DEV)], landed.at[me], local_sem.at[3]
    )
    each_peer(lambda step: out_copy(step).start())
    own_out.start()
    own_out.wait()
    each_peer(lambda step: out_copy(step).wait_recv())
    for slot in range(KT_DEV * ranks):
        slots[slot] = natural[owner[slot]]
    each_peer(lambda step: back_copy(step).start())
    own_back.start()
    own_back.wait()

    def drain(e, _):
        @pl.when(inside(e))
        def _():
            level = (line + offset(e)) * 4
            for band in (1, 0):
                along_line(level + spot, band, e, wait_send)
                shard(level + spot, band, 2, first_rank).wait_send()
                shard(level + spot, band, 3, second_rank).wait_send()
            shard(level + first, 0, 3, second_rank).wait_send()
            along_line(level + across, 1, e, wait_send)

        return 0

    shard(first_rank, 1, 3, second_rank).wait_send()
    lax.fori_loop(0, last, drain, 0)
    for step in range(1, pairs):
        panel_copy(step).wait_send()
    each_peer(lambda step: out_copy(step).wait_send())
    each_peer(lambda step: back_copy(step).wait_recv())
    for i in range(ranks):
        for n in range(KT_DEV):
            out[i * part : (i + 1) * part, n * TILE : (n + 1) * TILE] = landed[i, n].astype(out.dtype)
    each_peer(lambda step: back_copy(step).wait_send())


def ladder(ranks, pairs, amplitudes, tile_owner, integrals, screening):
    rows, width = amplitudes.shape
    tiles = integrals.shape[0] // TILE
    vmem, smem = pl.BlockSpec(memory_space=pltpu.VMEM), pl.BlockSpec(memory_space=pltpu.SMEM)
    hbm = pl.BlockSpec(memory_space=pl.ANY)
    part = rows // ranks
    return pl.pallas_call(
        functools.partial(ladder_kernel, ranks, pairs),
        out_shape=jax.ShapeDtypeStruct((rows, width), jnp.float32),
        in_specs=[smem, smem, hbm, hbm],
        out_specs=vmem,
        scratch_shapes=[
            pltpu.VMEM((ranks, rows, width), jnp.bfloat16),
            pltpu.VMEM((tiles * pairs, TILE, width), jnp.bfloat16),
            pltpu.VMEM((KT_DEV, rows, width), jnp.bfloat16),
            pltpu.VMEM((rows, width), jnp.float32),
            pltpu.VMEM((ranks, KT_DEV, part, TILE), jnp.bfloat16),
            pltpu.VMEM((ranks * KT_DEV, part, TILE), jnp.bfloat16),
            pltpu.VMEM((ranks * KT_DEV, part, TILE), jnp.bfloat16),
            pltpu.VMEM((ranks, KT_DEV, part, TILE), jnp.bfloat16),
            pltpu.SemaphoreType.DMA((4,)),
            pltpu.SemaphoreType.DMA((2, 4, ranks)),
            pltpu.SemaphoreType.DMA((2, ranks)),
            pltpu.SemaphoreType.DMA((pairs - 1,)),
            pltpu.SemaphoreType.DMA((pairs - 1,)),
            pltpu.SemaphoreType.DMA((ranks - 1,)),
            pltpu.SemaphoreType.DMA((ranks - 1,)),
            pltpu.SemaphoreType.DMA((ranks - 1,)),
            pltpu.SemaphoreType.DMA((ranks - 1,)),
        ],
        compiler_params=pltpu.CompilerParams(
            collective_id=0, has_side_effects=True, vmem_limit_bytes=62 * 1024 * 1024
        ),
    )(tile_owner, screening, amplitudes, integrals.reshape(tiles, TILE, width))


def local(ranks, pairs, amplitudes, tile_owner, integrals, screening, occ_energy, virt_energy):
    pair_local = amplitudes.shape[0]
    tile_count = tile_owner.shape[0]
    width = KT_DEV * TILE
    column = lax.axis_index("vcol")
    owned_tiles = lax.dynamic_slice_in_dim(tile_owner, column * KT_DEV, KT_DEV, 0)
    ladder_owned = ladder(ranks, pairs, amplitudes, tile_owner, integrals, screening)
    virt_owned = jnp.dot(
        one_hot(owned_tiles, tile_count),
        virt_energy.reshape(tile_count, TILE),
        precision=lax.Precision.HIGHEST,
    ).reshape(width)
    residual = ladder_owned + (virt_owned[None, :] - occ_energy[:, None]) * amplitudes.astype(
        jnp.float32
    )
    return residual.astype(jnp.bfloat16)


def solution(mesh):
    return jax.shard_map(
        functools.partial(local, mesh.shape["vcol"], mesh.shape["pair"]),
        mesh=mesh,
        in_specs=(P("pair", "vcol"), P(), P("pair", "vcol"), P("pair", None, None), P("pair"), P()),
        out_specs=P("pair", "vcol"),
        check_vma=False,
    )
```

profile of v0, /device:TPU:0, one launch (start us, length us, event | category | flops | bytes accessed | tf_op | source)
XLA Modules:
  0.0 70.9 jit_solution(8663564225694767419)
XLA Ops:
  0.0 0.0 copy-start
  0.0 0.0 copy-start.3
  0.0 0.7 copy-done.3
  0.7 0.1 dynamic_slice.3
  0.7 0.0 copy-done
  0.7 0.2 convolution_bitcast_fusion
  0.9 0.0 copy-start.1
  0.9 0.0 copy-start.2
  0.9 67.9 %shard_map.64 = f32[640,256]{1,0:T(8,128)} custom-call(s32[32]{0:T(128)} %owner.1, s32[10,32,32]{2,1,0:T(8,128)} %screen.1, bf16[640,256]{1,0:T(8,128)(2,1)} %amps.1, bf16[16,128,256]{2,1,0:T(8,128)(2,1)} %bitcast.6), custom_call_target="tpu_custom_call" | custom-call | tf_op jit(solution)/shard_map/pallas_call | solution.py:284
  68.9 0.0 copy-done.1
  68.9 0.0 copy-done.2
  68.9 2.0 %add_convert_fusion = bf16[640,256]{1,0:T(8,128)(2,1)} fusion(f32[640,256]{1,0:T(8,128)} %shard_map.64, bf16[640,256]{1,0:T(8,128)(2,1)S(1)} %copy-done.1, f32[640]{0:T(1024)S(1)} %copy-done.2, f32[256]{0:T(256)S(1)} %convolution_bitcast_fusion), kind=kLoop, calls=%fused_computation.1 | loop fusion | flops 819200 | bytes 1314304 | tf_op jit(solution)/shard_map/convert_element_type | solution.py:329
Async XLA Ops:
  0.0 0.7 %copy-start = (f32[4096]{0:T(1024)S(1)}, f32[4096]{0:T(1024)}, u32[]{:S(2)}) copy-start(f32[4096]{0:T(1024)} %param.11) | copy-start | bytes 49156
  0.0 0.7 copy-start.3
  0.9 67.9 %copy-start.1 = (bf16[640,256]{1,0:T(8,128)(2,1)S(1)}, bf16[640,256]{1,0:T(8,128)(2,1)}, u32[]{:S(2)}) copy-start(bf16[640,256]{1,0:T(8,128)(2,1)} %amps.1) | copy-start | bytes 983044
  0.9 67.9 %copy-start.2 = (f32[640]{0:T(1024)S(1)}, f32[640]{0:T(1024)}, u32[]{:S(2)}) copy-start(f32[640]{0:T(1024)} %param.10) | copy-start | bytes 7684
where the time goes:
time: 71.4 us; the launch traced here: 70.9 us
  Pallas kernels  67.9 us (95%)
  other arithmetic  1.99 us (3%)
  local copies, waits for them, and re-layouts  0.75 us (1%)
    pallas_call x1, Pallas kernels, ladder(): pl.pallas_call(functools.partial(ladder_kernel, ranks, pairs), out_shape=...  67.9 us
    convert_element_type x1, other arithmetic, local(): return residual.astype(jnp.bfloat16)  1.99 us

commit v1 on v0

v1 whole, which is shorter than its diff:
```python
import functools

import jax
import jax.numpy as jnp
from jax import lax
from jax.experimental import pallas as pl
from jax.experimental.pallas import tpu as pltpu
from jax.sharding import PartitionSpec as P

TILE = 128
PBLK = 64
KT_DEV = 2
MESH = pl.DeviceIdType.MESH
UP, DOWN, BESIDE, PARTNER = 0, 1, 2, 3


def one_hot(indices, length):
    return (indices[:, None] == jnp.arange(length, dtype=jnp.int32)[None, :]).astype(jnp.float32)


def ladder_kernel(
    ranks, pairs, owner, screen, amps, ints, out,
    gath, panel, stage, far, lhs, acc, parts, natural, slots, landed,
    local_sem, send_sem, recv_sem, pair_send, pair_recv, far_send, far_recv, pass_send, pass_recv,
    out_send, out_recv, back_send, back_recv,
):
    length = ranks // 4
    plane = ranks // 2
    me = lax.axis_index("vcol")
    core = lax.axis_index("pair")
    line, spot = me // 4, me % 4
    hi, lo = spot // 2, spot % 2
    beside = line * 4 + hi * 2 + (1 - lo)
    partner = line * 4 + (1 - hi) * 2 + lo
    has_up, has_down = line < length - 1, line > 0
    half = gath.shape[1]
    blocks = half // PBLK
    tiles = ints.shape[0]
    chunks = stage.shape[0]
    per_line = chunks // length

    own_amps = pltpu.make_async_copy(amps.at[pl.ds(hi * half, half)], gath.at[me], local_sem.at[0])
    own_ints = pltpu.make_async_copy(ints, panel.at[pl.ds(core * tiles, tiles)], local_sem.at[1])
    own_amps.start()
    own_ints.start()

    barrier = pltpu.get_barrier_semaphore()

    def greet_step(step, _):
        pl.semaphore_signal(
            barrier, inc=1, device_id={"vcol": (me + step) % ranks}, device_id_type=MESH
        )
        return 0

    lax.fori_loop(1, ranks, greet_step, 0)
    for step in range(1, pairs):
        pl.semaphore_signal(
            barrier, inc=1, device_id={"pair": (core + step) % pairs}, device_id_type=MESH
        )
    pl.semaphore_wait(barrier, ranks - 1 + pairs - 1)

    cut = (blocks * 3 // 5) * PBLK
    bands = ((0, cut), (cut, half))

    def first_copy(band, way, target):
        low, high = bands[band]
        base = (1 - hi) * half if way == PARTNER else hi * half
        return pltpu.make_async_remote_copy(
            src_ref=amps.at[pl.ds(base + low, high - low)],
            dst_ref=gath.at[me, pl.ds(low, high - low)],
            send_sem=send_sem.at[band, way, me], recv_sem=recv_sem.at[band, me],
            device_id={"vcol": target}, device_id_type=MESH,
        )

    def relay(source, band, way, target):
        low, high = bands[band]
        place = gath.at[source, pl.ds(low, high - low)]
        return pltpu.make_async_remote_copy(
            src_ref=place, dst_ref=place,
            send_sem=send_sem.at[band, way, source], recv_sem=recv_sem.at[band, source],
            device_id={"vcol": target}, device_id_type=MESH,
        )

    def arrived(source, band):
        relay(source, band, BESIDE, beside).wait_recv()

    def panel_copy(step):
        return pltpu.make_async_remote_copy(
            src_ref=ints, dst_ref=panel.at[pl.ds(core * tiles, tiles)],
            send_sem=pair_send.at[step - 1], recv_sem=pair_recv.at[step - 1],
            device_id={"pair": (core + step) % pairs}, device_id_type=MESH,
        )

    def far_copy(chunk):
        return pltpu.make_async_remote_copy(
            src_ref=stage.at[chunk], dst_ref=far.at[chunk * pairs + core],
            send_sem=far_send.at[chunk], recv_sem=far_recv.at[chunk],
            device_id={"vcol": partner}, device_id_type=MESH,
        )

    def pass_copy(chunk, step, holder):
        place = far.at[chunk * pairs + holder]
        return pltpu.make_async_remote_copy(
            src_ref=place, dst_ref=place,
            send_sem=pass_send.at[step - 1, chunk], recv_sem=pass_recv.at[step - 1, chunk],
            device_id={"pair": (core + step) % pairs}, device_id_type=MESH,
        )

    def multiply(source, side):
        tile_pair = (owner[KT_DEV * source], owner[KT_DEV * source + 1])
        home = partner if side else me
        for slot, tile in enumerate(tile_pair):
            columns = slice(slot * TILE, (slot + 1) * TILE)
            for block in range(blocks):
                part = slice(block * PBLK, (block + 1) * PBLK)
                value = gath[source, part, columns]
                for n in range(KT_DEV):
                    mark = screen[hi * blocks + block, tile, KT_DEV * home + n].astype(jnp.float32)
                    lhs[n, part, columns] = value * jnp.full(value.shape, mark, jnp.float32).astype(
                        value.dtype
                    )
        if side:
            right = jnp.concatenate([far[KT_DEV * source], far[KT_DEV * source + 1]], axis=0)
        else:
            right = jnp.concatenate([panel[tile] for tile in tile_pair], axis=0)
        for n in range(KT_DEV):
            columns = slice(n * TILE, (n + 1) * TILE)
            place = slice((KT_DEV * side + n) * TILE, (KT_DEV * side + n + 1) * TILE)
            acc[:, place] += jnp.dot(lhs[n], right[:, columns], preferred_element_type=jnp.float32)

    def offset(e):
        return ((e + 1) // 2) * (1 - 2 * (e % 2))

    def inside(e):
        at = line + offset(e)
        return (at >= 0) & (at < length)

    def goes_up(e):
        return ((e % 2 == 1) | (e == 0)) & has_up

    def goes_down(e):
        return (e % 2 == 0) & has_down

    def forward(source, band, e, action):
        @pl.when(goes_up(e))
        def _():
            action(relay(source, band, UP, me + 4))

        @pl.when(goes_down(e))
        def _():
            action(relay(source, band, DOWN, me - 4))

        action(relay(source, band, BESIDE, beside))

    def start(copy):
        copy.start()

    def wait_send(copy):
        copy.wait_send()

    def first_copies(action):
        for band in (0, 1):
            action(first_copy(band, PARTNER, partner))

            @pl.when(has_up)
            def _():
                action(first_copy(band, UP, me + 4))

            @pl.when(has_down)
            def _():
                action(first_copy(band, DOWN, me - 4))

            action(first_copy(band, BESIDE, beside))

    first_copies(start)
    for step in range(1, pairs):
        panel_copy(step).start()
    acc[...] = jnp.zeros_like(acc)
    own_ints.wait()
    for step in range(1, pairs):
        panel_copy(step).wait_recv()

    last = 2 * length - 1

    def on_line(e, action):
        @pl.when(inside(e))
        def _():
            for i in range(per_line):
                action((line + offset(e)) * per_line + i)

    def stage_line(e, _):
        def fill(chunk):
            stage[chunk] = panel[owner[chunk * pairs + core]]

        on_line(e, fill)
        return 0

    def send_line(e, _):
        on_line(e, lambda chunk: far_copy(chunk).start())
        return 0

    lax.fori_loop(0, last, stage_line, 0)
    lax.fori_loop(0, last, send_line, 0)
    for band in (0, 1):
        arrived(partner, band)
        forward(partner, band, jnp.int32(0), start)
    own_amps.wait()
    multiply(me, 0)
    multiply(partner, 0)

    def on_step(e, _):
        at = line + offset(e)

        @pl.when((e < last) & inside(e))
        def _():
            for h in (hi, 1 - hi):
                for band in (0, 1):
                    arrived(at * 4 + h * 2 + lo, band)
                    forward(at * 4 + h * 2 + lo, band, e, start)

        late = e - 2
        behind = line + offset(late)

        @pl.when((late >= 0) & inside(late))
        def _():
            for i in range(per_line):
                chunk = behind * per_line + i
                far_copy(chunk).wait_recv()
                for step in range(1, pairs):
                    pass_copy(chunk, step, core).start()

        @pl.when((e < last) & inside(e))
        def _():
            for h in range(2):
                multiply(at * 4 + h * 2 + lo, 0)

        @pl.when((late >= 0) & inside(late))
        def _():
            for h in (hi, 1 - hi):
                source = behind * 4 + h * 2 + (1 - lo)
                for band in (0, 1):
                    arrived(source, band)
                multiply(source, 0)
            for i in range(per_line):
                for step in range(1, pairs):
                    pass_copy(
                        behind * per_line + i, step, (core + pairs - step) % pairs
                    ).wait_recv()
            for place in range(4):
                multiply(behind * 4 + place, 1)

        return 0

    lax.fori_loop(1, last + 2, on_step, 0)

    part = half // plane
    width = KT_DEV * 2
    spot_in_plane = line * 2 + lo
    for i in range(plane):
        for n in range(width):
            parts[i, n] = acc[i * part : (i + 1) * part, n * TILE : (n + 1) * TILE].astype(
                parts.dtype
            )

    def out_copy(step):
        target = (spot_in_plane + step) % plane
        return pltpu.make_async_remote_copy(
            src_ref=parts.at[target], dst_ref=natural.at[spot_in_plane],
            send_sem=out_send.at[step - 1], recv_sem=out_recv.at[step - 1],
            device_id={"vcol": (target // 2) * 4 + hi * 2 + target % 2}, device_id_type=MESH,
        )

    def back_copy(step):
        target = (me + step) % ranks
        return pltpu.make_async_remote_copy(
            src_ref=slots.at[target], dst_ref=landed.at[me],
            send_sem=back_send.at[step - 1], recv_sem=back_recv.at[step - 1],
            device_id={"vcol": target}, device_id_type=MESH,
        )

    def each(count, action):
        def body(step, _):
            action(step)
            return 0

        lax.fori_loop(1, count, body, 0)

    each(plane, lambda step: out_copy(step).start())
    own_out = pltpu.make_async_copy(
        parts.at[spot_in_plane], natural.at[spot_in_plane], local_sem.at[2]
    )
    own_out.start()
    own_out.wait()
    each(plane, lambda step: out_copy(step).wait_recv())
    for j in range(ranks):
        for n in range(KT_DEV):
            tile = owner[KT_DEV * j + n]
            chip, odd = tile // KT_DEV, tile % KT_DEV
            row, col = (chip % 4) // 2, chip % 2
            slots[j, n] = natural[(chip // 4) * 2 + col, ((row + hi) % 2) * KT_DEV + odd]
    each(ranks, lambda step: back_copy(step).start())
    own_back = pltpu.make_async_copy(slots.at[me], landed.at[me], local_sem.at[3])
    own_back.start()
    own_back.wait()

    first_copies(wait_send)
    for band in (0, 1):
        forward(partner, band, jnp.int32(0), wait_send)

    def drain(e, _):
        @pl.when((e > 0) & inside(e))
        def _():
            for h in range(2):
                for band in (0, 1):
                    forward((line + offset(e)) * 4 + h * 2 + lo, band, e, wait_send)

        def close(chunk):
            far_copy(chunk).wait_send()
            for step in range(1, pairs):
                pass_copy(chunk, step, core).wait_send()

        on_line(e, close)
        return 0

    lax.fori_loop(0, last, drain, 0)
    for step in range(1, pairs):
        panel_copy(step).wait_send()
    each(plane, lambda step: out_copy(step).wait_send())
    each(ranks, lambda step: back_copy(step).wait_recv())
    for j in range(ranks):
        base = ((j % 4) // 2) * half + ((j // 4) * 2 + j % 2) * part
        for n in range(KT_DEV):
            out[base : base + part, n * TILE : (n + 1) * TILE] = landed[j, n].astype(out.dtype)
    each(ranks, lambda step: back_copy(step).wait_send())


def ladder(ranks, pairs, amplitudes, tile_owner, integrals, screening):
    rows, width = amplitudes.shape
    tiles = integrals.shape[0] // TILE
    half, plane = rows // 2, ranks // 2
    chunks = KT_DEV * ranks // pairs
    vmem, smem = pl.BlockSpec(memory_space=pltpu.VMEM), pl.BlockSpec(memory_space=pltpu.SMEM)
    hbm = pl.BlockSpec(memory_space=pl.ANY)
    part = half // plane
    dma = pltpu.SemaphoreType.DMA
    return pl.pallas_call(
        functools.partial(ladder_kernel, ranks, pairs),
        out_shape=jax.ShapeDtypeStruct((rows, width), jnp.float32),
        in_specs=[smem, smem, hbm, hbm],
        out_specs=vmem,
        scratch_shapes=[
            pltpu.VMEM((ranks, half, width), jnp.bfloat16),
            pltpu.VMEM((tiles * pairs, TILE, width), jnp.bfloat16),
            pltpu.VMEM((chunks, TILE, width), jnp.bfloat16),
            pltpu.VMEM((KT_DEV * ranks, TILE, width), jnp.bfloat16),
            pltpu.VMEM((KT_DEV, half, width), jnp.bfloat16),
            pltpu.VMEM((half, 2 * width), jnp.float32),
            pltpu.VMEM((plane, 2 * KT_DEV, part, TILE), jnp.bfloat16),
            pltpu.VMEM((plane, 2 * KT_DEV, part, TILE), jnp.bfloat16),
            pltpu.VMEM((ranks, KT_DEV, part, TILE), jnp.bfloat16),
            pltpu.VMEM((ranks, KT_DEV, part, TILE), jnp.bfloat16),
            dma((4,)),
            dma((2, 4, ranks)),
            dma((2, ranks)),
            dma((pairs - 1,)),
            dma((pairs - 1,)),
            dma((chunks,)),
            dma((chunks,)),
            dma((pairs - 1, chunks)),
            dma((pairs - 1, chunks)),
            dma((plane - 1,)),
            dma((plane - 1,)),
            dma((ranks - 1,)),
            dma((ranks - 1,)),
        ],
        compiler_params=pltpu.CompilerParams(
            collective_id=0, has_side_effects=True, vmem_limit_bytes=62 * 1024 * 1024
        ),
    )(tile_owner, screening, amplitudes, integrals.reshape(tiles, TILE, width))


def local(ranks, pairs, amplitudes, tile_owner, integrals, screening, occ_energy, virt_energy):
    tile_count = tile_owner.shape[0]
    width = KT_DEV * TILE
    column = lax.axis_index("vcol")
    owned_tiles = lax.dynamic_slice_in_dim(tile_owner, column * KT_DEV, KT_DEV, 0)
    ladder_owned = ladder(ranks, pairs, amplitudes, tile_owner, integrals, screening)
    virt_owned = jnp.dot(
        one_hot(owned_tiles, tile_count),
        virt_energy.reshape(tile_count, TILE),
        precision=lax.Precision.HIGHEST,
    ).reshape(width)
    residual = ladder_owned + (virt_owned[None, :] - occ_energy[:, None]) * amplitudes.astype(
        jnp.float32
    )
    return residual.astype(jnp.bfloat16)


def solution(mesh):
    return jax.shard_map(
        functools.partial(local, mesh.shape["vcol"], mesh.shape["pair"]),
        mesh=mesh,
        in_specs=(P("pair", "vcol"), P(), P("pair", "vcol"), P("pair", None, None), P("pair"), P()),
        out_specs=P("pair", "vcol"),
        check_vma=False,
    )
```

time: 71.4 us -> 63 us (0.88)
  Pallas kernels: 67.9 us -> 59.8 us
    pallas_call x1, Pallas kernels: 67.9 us -> 59.8 us  [ladder(): pl.pallas_call(functools.partial(ladder_kernel, ranks, pairs), out_shape=...]
where the time goes in v1:
time: 63 us; the launch traced here: 62.7 us
  Pallas kernels  59.8 us (95%)
  other arithmetic  1.99 us (3%)
  local copies, waits for them, and re-layouts  0.75 us (1%)
    pallas_call x1, Pallas kernels, ladder(): pl.pallas_call(functools.partial(ladder_kernel, ranks, pairs), out_shape=...  59.8 us
    convert_element_type x1, other arithmetic, local(): return residual.astype(jnp.bfloat16)  1.99 us

profile of v1, /device:TPU:0, one launch (start us, length us, event | category | flops | bytes accessed | tf_op | source)
XLA Modules:
  0.0 62.7 jit_solution(11293871829033961392)
XLA Ops:
  0.0 0.0 copy-start
  0.0 0.0 copy-start.3
  0.0 0.7 %copy-done.3 = s32[32]{0:T(128)S(1)} copy-done((s32[32]{0:T(128)S(1)}, s32[32]{0:T(128)}, u32[]{:S(2)}) %copy-start.3) | copy-done | bytes 152
  0.7 0.1 dynamic_slice.3
  0.7 0.0 copy-done
  0.7 0.2 convolution_bitcast_fusion
  0.9 0.0 copy-start.1
  0.9 0.0 copy-start.2
  0.9 59.8 %shard_map.64 = f32[640,256]{1,0:T(8,128)} custom-call(s32[32]{0:T(128)} %owner.1, s32[10,32,32]{2,1,0:T(8,128)} %screen.1, bf16[640,256]{1,0:T(8,128)(2,1)} %amps.1, bf16[16,128,256]{2,1,0:T(8,128)(2,1)} %bitcast.6), custom_call_target="tpu_custom_call" | custom-call | tf_op jit(solution)/shard_map/pallas_call | solution.py:346
  60.7 0.0 copy-done.1
  60.7 0.0 copy-done.2
  60.7 2.0 %add_convert_fusion = bf16[640,256]{1,0:T(8,128)(2,1)} fusion(f32[640,256]{1,0:T(8,128)} %shard_map.64, bf16[640,256]{1,0:T(8,128)(2,1)S(1)} %copy-done.1, f32[640]{0:T(1024)S(1)} %copy-done.2, f32[256]{0:T(256)S(1)} %convolution_bitcast_fusion), kind=kLoop, calls=%fused_computation.1 | loop fusion | flops 819200 | bytes 1314304 | tf_op jit(solution)/shard_map/convert_element_type | solution.py:396
Async XLA Ops:
  0.0 0.7 %copy-start = (f32[4096]{0:T(1024)S(1)}, f32[4096]{0:T(1024)}, u32[]{:S(2)}) copy-start(f32[4096]{0:T(1024)} %param.11) | copy-start | bytes 49156
  0.0 0.7 %copy-start.3 = (s32[32]{0:T(128)S(1)}, s32[32]{0:T(128)}, u32[]{:S(2)}) copy-start(s32[32]{0:T(128)} %owner.1) | copy-start | bytes 388
  0.9 59.8 %copy-start.1 = (bf16[640,256]{1,0:T(8,128)(2,1)S(1)}, bf16[640,256]{1,0:T(8,128)(2,1)}, u32[]{:S(2)}) copy-start(bf16[640,256]{1,0:T(8,128)(2,1)} %amps.1) | copy-start | bytes 983044
  0.9 59.8 %copy-start.2 = (f32[640]{0:T(1024)S(1)}, f32[640]{0:T(1024)}, u32[]{:S(2)}) copy-start(f32[640]{0:T(1024)} %param.10) | copy-start | bytes 7684

commit v2 on v1

v2 whole, which is shorter than its diff:
```python
import functools

import jax
import jax.numpy as jnp
from jax import lax
from jax.experimental import pallas as pl
from jax.experimental.pallas import tpu as pltpu
from jax.sharding import PartitionSpec as P

TILE = 128
PBLK = 64
KT_DEV = 2
MESH = pl.DeviceIdType.MESH
UP, DOWN, BESIDE, PARTNER = 0, 1, 2, 3


def band_edges(half):
    cut = (half // PBLK * 3 // 5) * PBLK
    return ((0, cut), (cut, half))


def ladder_kernel(
    ranks, pairs, amps, owner_in, ints, screen_in, occ_in, virt_in, out,
    owner, screen, occ, virt, mine, base, gath, panel, stage, far, lhs, acc,
    parts0, parts1, natural0, natural1, slots0, slots1, landed0, landed1,
    local_sem, send_sem, recv_sem, pair_send, pair_recv, far_send, far_recv, pass_send, pass_recv,
    out_send, out_recv, back_send, back_recv,
):
    length = ranks // 4
    plane = ranks // 2
    groups = pairs // 2
    me = lax.axis_index("vcol")
    core = lax.axis_index("pair")
    line, spot = me // 4, me % 4
    hi, lo = spot // 2, spot % 2
    beside = line * 4 + hi * 2 + (1 - lo)
    partner = line * 4 + (1 - hi) * 2 + lo
    has_up, has_down = line < length - 1, line > 0
    half = gath.shape[1]
    blocks = half // PBLK
    tiles = ints.shape[0]
    bands = band_edges(half)

    def load(index, source, target):
        return pltpu.make_async_copy(source, target, local_sem.at[index])

    own_ints = load(0, ints, panel.at[pl.ds(core * tiles, tiles)])
    own_amps = load(1, amps.at[pl.ds(hi * half, half)], gath.at[me])
    get_owner = load(2, owner_in, owner)
    get_screen = load(3, screen_in.at[pl.ds(hi * blocks, blocks)], screen)
    get_occ = load(4, occ_in, occ)
    get_virt = load(5, virt_in, virt)
    get_mine = load(6, amps, mine)
    loads = (get_owner, own_ints, get_screen, own_amps, get_occ, get_virt, get_mine)

    barrier = pltpu.get_barrier_semaphore()

    def greet(target):
        pl.semaphore_signal(barrier, inc=1, device_id={"vcol": target}, device_id_type=MESH)

    greet(beside)
    greet(partner)
    pl.when(has_up)(lambda: greet(me + 4))
    pl.when(has_down)(lambda: greet(me - 4))
    for step in range(1, pairs):
        pl.semaphore_signal(
            barrier, inc=1, device_id={"pair": (core + step) % pairs}, device_id_type=MESH
        )
    for copy in loads:
        copy.start()
    pl.semaphore_wait(
        barrier, pairs + 1 + has_up.astype(jnp.int32) + has_down.astype(jnp.int32)
    )

    def first_copy(band, way, target):
        low, high = bands[band]
        start_row = (1 - hi) * half if way == PARTNER else hi * half
        return pltpu.make_async_remote_copy(
            src_ref=amps.at[pl.ds(start_row + low, high - low)],
            dst_ref=gath.at[me, pl.ds(low, high - low)],
            send_sem=send_sem.at[band, way, me], recv_sem=recv_sem.at[band, me],
            device_id={"vcol": target}, device_id_type=MESH,
        )

    def relay(source, band, way, target):
        low, high = bands[band]
        place = gath.at[source, pl.ds(low, high - low)]
        return pltpu.make_async_remote_copy(
            src_ref=place, dst_ref=place,
            send_sem=send_sem.at[band, way, source], recv_sem=recv_sem.at[band, source],
            device_id={"vcol": target}, device_id_type=MESH,
        )

    def panel_copy(step):
        return pltpu.make_async_remote_copy(
            src_ref=ints, dst_ref=panel.at[pl.ds(core * tiles, tiles)],
            send_sem=pair_send.at[step - 1], recv_sem=pair_recv.at[step - 1],
            device_id={"pair": (core + step) % pairs}, device_id_type=MESH,
        )

    def far_copy(source):
        return pltpu.make_async_remote_copy(
            src_ref=stage.at[source], dst_ref=far.at[KT_DEV * source + core % 2],
            send_sem=far_send.at[source], recv_sem=far_recv.at[source],
            device_id={"vcol": partner}, device_id_type=MESH,
        )

    def pass_copy(source, step, holder):
        slot = KT_DEV * source + holder % 2
        return pltpu.make_async_remote_copy(
            src_ref=far.at[slot], dst_ref=far.at[slot],
            send_sem=pass_send.at[step - 1, slot], recv_sem=pass_recv.at[slot],
            device_id={"pair": (core + step) % pairs}, device_id_type=MESH,
        )

    def if_holder(source, holder, action):
        if groups == 1:
            action()
        else:
            pl.when(source % groups == holder // 2)(action)

    def start(copy):
        copy.start()

    def wait_send(copy):
        copy.wait_send()

    def inside(at):
        return (at >= 0) & (at < length)

    def skipped(at):
        low = jnp.where(at % 2 == 0, at + 2, at - 1)
        high = jnp.where(at % 2 == 0, at + 1, at - 2)
        return jnp.where(at < length // 2, low, high)

    mate = line + 1 - 2 * (line % 2)
    skip, mate_skip = skipped(line), skipped(mate)

    def on_level(level, action):
        odd = level % 2
        h = hi + odd - 2 * hi * odd
        for x in (0, 1):
            d = level // 2 - x
            for away in (-1, 1):
                at = line + away * d
                valid = (d > 0 if away < 0 else d >= 0) & inside(at)
                pl.when(valid)(functools.partial(action, x, at, h, odd))

    def unit(at, h, x):
        return at * 4 + h * 2 + (1 - lo if x else lo)

    def onward(x, at, h, odd, band, action):
        source = unit(at, h, x)
        if x == 0:
            pl.when((at <= line) & has_up)(lambda: action(relay(source, band, UP, me + 4)))
            pl.when((at >= line) & has_down)(lambda: action(relay(source, band, DOWN, me - 4)))
            pl.when((at != skip) | (odd == 0))(
                lambda: action(relay(source, band, BESIDE, beside))
            )
        else:
            wanted = (at == mate_skip) & (odd == 1)
            pl.when(wanted & (mate > line))(lambda: action(relay(source, band, UP, me + 4)))
            pl.when(wanted & (mate < line))(lambda: action(relay(source, band, DOWN, me - 4)))

    def first_copies(action):
        for band in (0, 1):
            action(first_copy(band, PARTNER, partner))
            pl.when(has_up)(lambda: action(first_copy(band, UP, me + 4)))
            pl.when(has_down)(lambda: action(first_copy(band, DOWN, me - 4)))
            action(first_copy(band, BESIDE, beside))

    def multiply(source, side, first, stop):
        tile_pair = (owner[KT_DEV * source], owner[KT_DEV * source + 1])
        home = partner if side else me
        rows = slice(first * PBLK, stop * PBLK)
        for slot, tile in enumerate(tile_pair):
            columns = slice(slot * TILE, (slot + 1) * TILE)
            for block in range(first, stop):
                part = slice(block * PBLK, (block + 1) * PBLK)
                value = gath[source, part, columns]
                for n in range(KT_DEV):
                    mark = screen[block, tile, KT_DEV * home + n].astype(jnp.float32)
                    lhs[n, part, columns] = value * jnp.full(value.shape, mark, jnp.float32).astype(
                        value.dtype
                    )
        if side:
            right = jnp.concatenate([far[KT_DEV * source], far[KT_DEV * source + 1]], axis=0)
        else:
            right = jnp.concatenate([panel[tile] for tile in tile_pair], axis=0)
        for n in range(KT_DEV):
            columns = slice(n * TILE, (n + 1) * TILE)
            place = slice((KT_DEV * side + n) * TILE, (KT_DEV * side + n + 1) * TILE)
            acc[rows, place] += jnp.dot(
                lhs[n, rows], right[:, columns], preferred_element_type=jnp.float32
            )

    first_copies(start)
    for step in range(1, pairs):
        panel_copy(step).start()
    acc[...] = jnp.zeros_like(acc)
    get_owner.wait()
    own_ints.wait()
    for step in range(1, pairs):
        panel_copy(step).wait_recv()

    def fill(source, _):
        if_holder(
            source, core,
            lambda: stage.__setitem__(source, panel[owner[KT_DEV * source + core % 2]]),
        )
        return 0

    def to_partner(action):
        def body(level, _):
            def send(x, at, h, odd):
                source = unit(at, 1 - h, x)
                if_holder(source, core, lambda: action(far_copy(source)))

            on_level(level, send)
            return 0

        lax.fori_loop(0, 2 * length + 2, body, 0)

    lax.fori_loop(0, ranks, fill, 0)
    to_partner(start)

    def pass_on(source):
        def go():
            far_copy(source).wait_recv()
            for step in range(1, pairs):
                pass_copy(source, step, core).start()

        if_holder(source, core, go)

    def passed(source):
        for step in range(1, pairs):
            holder = (core + step) % pairs
            if_holder(
                source, holder, lambda: pass_copy(source, step, holder).wait_recv()
            )

    def arrived(source, band):
        relay(source, band, BESIDE, beside).wait_recv()

    def far_whole(source):
        passed(source)
        multiply(source, 1, 0, blocks)

    get_screen.wait()
    own_amps.wait()
    multiply(me, 0, 0, blocks)

    def on_unit(action):
        return lambda x, at, h, odd: action(unit(at, h, x))

    def run_level(level, _):
        for band in (0, 1):

            def take(x, at, h, odd):
                arrived(unit(at, h, x), band)
                onward(x, at, h, odd, band, start)

            on_level(level, take)
        on_level(level - 1, on_unit(pass_on))
        on_level(level, on_unit(lambda source: multiply(source, 0, 0, blocks)))
        on_level(level - 1, on_unit(far_whole))
        return 0

    final = 2 * length + 1

    lax.fori_loop(1, final, run_level, 0)
    on_level(final - 1, on_unit(pass_on))
    on_level(final, on_unit(pass_on))
    on_level(final - 1, on_unit(far_whole))
    on_level(final, on_unit(passed))

    spot_in_plane = line * 2 + lo
    parts, natural = (parts0, parts1), (natural0, natural1)
    slots, landed = (slots0, slots1), (landed0, landed1)

    def out_copy(band, step):
        target = (spot_in_plane + step) % plane
        return pltpu.make_async_remote_copy(
            src_ref=parts[band].at[target], dst_ref=natural[band].at[spot_in_plane],
            send_sem=out_send.at[band, step - 1], recv_sem=out_recv.at[band, step - 1],
            device_id={"vcol": (target // 2) * 4 + hi * 2 + target % 2}, device_id_type=MESH,
        )

    def back_copy(band, step):
        target = (me + step) % ranks
        return pltpu.make_async_remote_copy(
            src_ref=slots[band].at[target], dst_ref=landed[band].at[me],
            send_sem=back_send.at[band, step - 1], recv_sem=back_recv.at[band, step - 1],
            device_id={"vcol": target}, device_id_type=MESH,
        )

    def each(count, action):
        def body(step, _):
            action(step)
            return 0

        lax.fori_loop(1, count, body, 0)

    for band in (0, 1):
        low, high = bands[band]

        def finish(source):
            arrived(source, band)
            for side in (0, 1):
                multiply(source, side, low // PBLK, high // PBLK)

        on_level(final, on_unit(finish))
        part = (high - low) // plane
        for i in range(plane):
            for n in range(2 * KT_DEV):
                parts[band][i, n] = acc[
                    low + i * part : low + (i + 1) * part, n * TILE : (n + 1) * TILE
                ].astype(jnp.bfloat16)
        each(plane, lambda step: out_copy(band, step).start())
        natural[band][spot_in_plane] = parts[band][spot_in_plane]

    get_occ.wait()
    get_virt.wait()
    get_mine.wait()
    rows = mine.shape[0]
    eye = lax.broadcasted_iota(jnp.int32, (TILE, TILE), 0) == lax.broadcasted_iota(
        jnp.int32, (TILE, TILE), 1
    )
    for g in range(rows // TILE):
        part = slice(g * TILE, (g + 1) * TILE)
        spread = jnp.broadcast_to(occ[g : g + 1, :], (TILE, TILE))
        column = jnp.sum(jnp.where(eye, spread, 0.0), axis=1, keepdims=True)
        for n in range(KT_DEV):
            columns = slice(n * TILE, (n + 1) * TILE)
            level = virt[pl.ds(owner[KT_DEV * me + n], 1), :]
            base[part, columns] = (level - column) * mine[part, columns].astype(jnp.float32)

    for band in (0, 1):
        each(plane, lambda step: out_copy(band, step).wait_recv())
        for j in range(ranks):
            for n in range(KT_DEV):
                tile = owner[KT_DEV * j + n]
                home, odd = tile // KT_DEV, tile % KT_DEV
                row, col = (home % 4) // 2, home % 2
                slots[band][j, n] = natural[band][
                    (home // 4) * 2 + col, ((row + hi) % 2) * KT_DEV + odd
                ]
        each(ranks, lambda step: back_copy(band, step).start())
        landed[band][me] = slots[band][me]

    first_copies(wait_send)

    def drain(level, _):
        for band in (0, 1):
            on_level(
                level, lambda x, at, h, odd: onward(x, at, h, odd, band, wait_send)
            )
        return 0

    lax.fori_loop(1, final + 1, drain, 0)
    to_partner(wait_send)

    def close(source, _):
        def go():
            for step in range(1, pairs):
                pass_copy(source, step, core).wait_send()

        if_holder(source, core, go)
        return 0

    lax.fori_loop(0, ranks, close, 0)
    for step in range(1, pairs):
        panel_copy(step).wait_send()
    for band in (0, 1):
        each(plane, lambda step: out_copy(band, step).wait_send())

    for band in (0, 1):
        low, high = bands[band]
        part = (high - low) // plane
        each(ranks, lambda step: back_copy(band, step).wait_recv())
        for j in range(ranks):
            at = ((j % 4) // 2) * half + low + ((j // 4) * 2 + j % 2) * part
            for n in range(KT_DEV):
                columns = slice(n * TILE, (n + 1) * TILE)
                out[at : at + part, columns] = (
                    landed[band][j, n].astype(jnp.float32) + base[at : at + part, columns]
                ).astype(out.dtype)
    for band in (0, 1):
        each(ranks, lambda step: back_copy(band, step).wait_send())


def local(ranks, pairs, amplitudes, tile_owner, integrals, screening, occ_energy, virt_energy):
    rows, width = amplitudes.shape
    tiles = integrals.shape[0] // TILE
    count = tile_owner.shape[0]
    half, plane = rows // 2, ranks // 2
    blocks = half // PBLK
    hbm = pl.BlockSpec(memory_space=pl.ANY)
    dma = pltpu.SemaphoreType.DMA
    sizes = [(high - low) // plane for low, high in band_edges(half)]

    def exchange(lead, tiles_each):
        return [pltpu.VMEM((lead, tiles_each, size, TILE), jnp.bfloat16) for size in sizes]

    return pl.pallas_call(
        functools.partial(ladder_kernel, ranks, pairs),
        out_shape=jax.ShapeDtypeStruct((rows, width), jnp.bfloat16),
        in_specs=[hbm] * 6,
        out_specs=pl.BlockSpec(memory_space=pltpu.VMEM),
        scratch_shapes=[
            pltpu.SMEM((count,), jnp.int32),
            pltpu.SMEM((blocks, count, count), jnp.int32),
            pltpu.VMEM((rows // TILE, TILE), jnp.float32),
            pltpu.VMEM((count, TILE), jnp.float32),
            pltpu.VMEM((rows, width), jnp.bfloat16),
            pltpu.VMEM((rows, width), jnp.float32),
            pltpu.VMEM((ranks, half, width), jnp.bfloat16),
            pltpu.VMEM((tiles * pairs, TILE, width), jnp.bfloat16),
            pltpu.VMEM((ranks, TILE, width), jnp.bfloat16),
            pltpu.VMEM((KT_DEV * ranks, TILE, width), jnp.bfloat16),
            pltpu.VMEM((KT_DEV, half, width), jnp.bfloat16),
            pltpu.VMEM((half, 2 * width), jnp.float32),
            *exchange(plane, 2 * KT_DEV),
            *exchange(plane, 2 * KT_DEV),
            *exchange(ranks, KT_DEV),
            *exchange(ranks, KT_DEV),
            dma((7,)),
            dma((2, 4, ranks)),
            dma((2, ranks)),
            dma((pairs - 1,)),
            dma((pairs - 1,)),
            dma((ranks,)),
            dma((ranks,)),
            dma((pairs - 1, KT_DEV * ranks)),
            dma((KT_DEV * ranks,)),
            dma((2, plane - 1)),
            dma((2, plane - 1)),
            dma((2, ranks - 1)),
            dma((2, ranks - 1)),
        ],
        compiler_params=pltpu.CompilerParams(
            collective_id=0, has_side_effects=True, vmem_limit_bytes=62 * 1024 * 1024
        ),
    )(
        amplitudes,
        tile_owner,
        integrals.reshape(tiles, TILE, width),
        screening,
        occ_energy.reshape(rows // TILE, TILE),
        virt_energy.reshape(count, TILE),
    )


def solution(mesh):
    return jax.shard_map(
        functools.partial(local, mesh.shape["vcol"], mesh.shape["pair"]),
        mesh=mesh,
        in_specs=(P("pair", "vcol"), P(), P("pair", "vcol"), P("pair", None, None), P("pair"), P()),
        out_specs=P("pair", "vcol"),
        check_vma=False,
    )
```

time: 63 us -> 59.8 us (0.949)
  other arithmetic: 1.99 us -> 0 us
  Pallas kernels: 59.8 us -> 57.9 us
  local copies, waits for them, and re-layouts: 0.75 us -> 1.72 us
    convert_element_type x1 -> x0, other arithmetic: 1.99 us -> none  [local(): return residual.astype(jnp.bfloat16)]
    pallas_call x1, Pallas kernels: 59.8 us -> 57.9 us  [local(): pl.pallas_call(functools.partial(ladder_kernel, ranks, pairs), out_shape=...]
    unnamed x8 -> x1, local copies, waits for them, and re-layouts: 0.68 us -> 1.72 us
where the time goes in v2:
time: 59.8 us; the launch traced here: 59.7 us
  Pallas kernels  57.9 us (97%)
  local copies, waits for them, and re-layouts  1.72 us (3%)
    pallas_call x1, Pallas kernels, local(): pl.pallas_call(functools.partial(ladder_kernel, ranks, pairs), out_shape=...  57.9 us
    unnamed x1, local copies, waits for them, and re-layouts  1.72 us

profile of v2, /device:TPU:0, one launch (start us, length us, event | category | flops | bytes accessed | tf_op | source)
XLA Modules:
  0.0 59.7 jit_solution(1956347438321629926)
XLA Ops:
  0.0 57.9 %shard_map.64 = bf16[640,256]{1,0:T(8,128)(2,1)} custom-call(bf16[640,256]{1,0:T(8,128)(2,1)} %amps.1, s32[32]{0:T(128)} %owner_in.1, bf16[16,128,256]{2,1,0:T(8,128)(2,1)} %bitcast.3, s32[10,32,32]{2,1,0:T(8,128)} %screen_in.1, f32[5,128]{1,0:T(8,128)} %bitcast.5, f32[32,128]{1,0:T(8,128)} %bitcast.4), custom_call_target="tpu_custom_call" | custom-call | tf_op jit(solution)/shard_map/pallas_call | solution.py:405
  57.9 1.7 %copy.8 = bf16[640,256]{1,0:T(8,128)(2,1)} copy(bf16[640,256]{1,0:T(8,128)(2,1)} %shard_map.64) | data formatting | bytes 655360

commit v3 on v2

--- a/solution.py
+++ b/solution.py
@@ -21,7 +21,7 @@
 
 def ladder_kernel(
     ranks, pairs, amps, owner_in, ints, screen_in, occ_in, virt_in, out,
-    owner, screen, occ, virt, mine, base, gath, panel, stage, far, lhs, acc,
+    owner, place, screen, occ, virt, mine, base, gath, panel, stage, far, lhs, acc,
     parts0, parts1, natural0, natural1, slots0, slots1, landed0, landed1,
     local_sem, send_sem, recv_sem, pair_send, pair_recv, far_send, far_recv, pass_send, pass_recv,
     out_send, out_recv, back_send, back_recv,
@@ -144,6 +144,8 @@
             for away in (-1, 1):
                 at = line + away * d
                 valid = (d > 0 if away < 0 else d >= 0) & inside(at)
+                if x == 1:
+                    valid = valid & ((at != skip) | (odd == 0))
                 pl.when(valid)(functools.partial(action, x, at, h, odd))
 
     def unit(at, h, x):
@@ -220,6 +222,8 @@
             return 0
 
         lax.fori_loop(0, 2 * length + 2, body, 0)
+        source = unit(skip, hi, 1)
+        if_holder(source, core, lambda: action(far_copy(source)))
 
     lax.fori_loop(0, ranks, fill, 0)
     to_partner(start)
@@ -246,6 +250,13 @@
         passed(source)
         multiply(source, 1, 0, blocks)
 
+    def find(slot, _):
+        tile = owner[slot]
+        row, col = (tile >> 2) & 1, (tile >> 1) & 1
+        place[slot] = (tile & -8) | (col << 2) | ((row ^ hi) << 1) | (tile & 1)
+        return 0
+
+    lax.fori_loop(0, KT_DEV * ranks, find, 0)
     get_screen.wait()
     own_amps.wait()
     multiply(me, 0, 0, blocks)
@@ -253,7 +264,7 @@
     def on_unit(action):
         return lambda x, at, h, odd: action(unit(at, h, x))
 
-    def run_level(level, _):
+    def relay_level(level):
         for band in (0, 1):
 
             def take(x, at, h, odd):
@@ -261,42 +272,72 @@
                 onward(x, at, h, odd, band, start)
 
             on_level(level, take)
+
+    def near_level(level):
+        on_level(level, on_unit(lambda source: multiply(source, 0, 0, blocks)))
+
+    def early_level(level, _):
+        relay_level(level)
         on_level(level - 1, on_unit(pass_on))
-        on_level(level, on_unit(lambda source: multiply(source, 0, 0, blocks)))
+        near_level(level)
         on_level(level - 1, on_unit(far_whole))
         return 0
 
+    def late_level(level, _):
+        on_level(level, on_unit(pass_on))
+        relay_level(level)
+        near_level(level)
+        on_level(level - 1, on_unit(far_whole))
+        return 0
+
     final = 2 * length + 1
-
-    lax.fori_loop(1, final, run_level, 0)
-    on_level(final - 1, on_unit(pass_on))
+    skipped_unit = unit(skip, 1 - hi, 1)
+
+    lax.fori_loop(1, final - 2, early_level, 0)
+    on_level(final - 3, on_unit(pass_on))
+    lax.fori_loop(final - 2, final, late_level, 0)
     on_level(final, on_unit(pass_on))
+    pass_on(skipped_unit)
     on_level(final - 1, on_unit(far_whole))
     on_level(final, on_unit(passed))
+    passed(skipped_unit)
 
     spot_in_plane = line * 2 + lo
     parts, natural = (parts0, parts1), (natural0, natural1)
     slots, landed = (slots0, slots1), (landed0, landed1)
 
-    def out_copy(band, step):
-        target = (spot_in_plane + step) % plane
-        return pltpu.make_async_remote_copy(
-            src_ref=parts[band].at[target], dst_ref=natural[band].at[spot_in_plane],
-            send_sem=out_send.at[band, step - 1], recv_sem=out_recv.at[band, step - 1],
+    def nearest(k, here, count):
+        wide = count // length
+        d = k // wide
+        low = jnp.minimum(line, length - 1 - line)
+        paired = line + ((d + 1) // 2) * (1 - 2 * (d % 2))
+        single = jnp.where(line < length // 2, d, length - 1 - d)
+        return jnp.where(d <= 2 * low, paired, single) * wide + (here + k) % wide
+
+    def out_copy(band, source, target):
+        return pltpu.make_async_remote_copy(
+            src_ref=parts[band].at[target], dst_ref=natural[band].at[pl.ds(source * 4, 4)],
+            send_sem=out_send.at[band, target], recv_sem=out_recv.at[band, source],
             device_id={"vcol": (target // 2) * 4 + hi * 2 + target % 2}, device_id_type=MESH,
         )
 
-    def back_copy(band, step):
-        target = (me + step) % ranks
-        return pltpu.make_async_remote_copy(
-            src_ref=slots[band].at[target], dst_ref=landed[band].at[me],
-            send_sem=back_send.at[band, step - 1], recv_sem=back_recv.at[band, step - 1],
+    def back_copy(band, source, target):
+        return pltpu.make_async_remote_copy(
+            src_ref=slots[band].at[target], dst_ref=landed[band].at[source],
+            send_sem=back_send.at[band, target], recv_sem=back_recv.at[band, source],
             device_id={"vcol": target}, device_id_type=MESH,
         )
 
-    def each(count, action):
+    def send_each(copy, band, here, count, action):
         def body(step, _):
-            action(step)
+            action(copy(band, here, nearest(count - step, here, count)))
+            return 0
+
+        lax.fori_loop(1, count, body, 0)
+
+    def take_each(copy, band, here, count):
+        def body(step, _):
+            copy(band, (here + step) % count, here).wait_recv()
             return 0
 
         lax.fori_loop(1, count, body, 0)
@@ -310,14 +351,15 @@
                 multiply(source, side, low // PBLK, high // PBLK)
 
         on_level(final, on_unit(finish))
+        finish(skipped_unit)
         part = (high - low) // plane
         for i in range(plane):
             for n in range(2 * KT_DEV):
                 parts[band][i, n] = acc[
                     low + i * part : low + (i + 1) * part, n * TILE : (n + 1) * TILE
                 ].astype(jnp.bfloat16)
-        each(plane, lambda step: out_copy(band, step).start())
-        natural[band][spot_in_plane] = parts[band][spot_in_plane]
+        send_each(out_copy, band, spot_in_plane, plane, start)
+        natural[band][pl.ds(spot_in_plane * 4, 4)] = parts[band][spot_in_plane]
 
     get_occ.wait()
     get_virt.wait()
@@ -336,16 +378,11 @@
             base[part, columns] = (level - column) * mine[part, columns].astype(jnp.float32)
 
     for band in (0, 1):
-        each(plane, lambda step: out_copy(band, step).wait_recv())
+        take_each(out_copy, band, spot_in_plane, plane)
         for j in range(ranks):
             for n in range(KT_DEV):
-                tile = owner[KT_DEV * j + n]
-                home, odd = tile // KT_DEV, tile % KT_DEV
-                row, col = (home % 4) // 2, home % 2
-                slots[band][j, n] = natural[band][
-                    (home // 4) * 2 + col, ((row + hi) % 2) * KT_DEV + odd
-                ]
-        each(ranks, lambda step: back_copy(band, step).start())
+                slots[band][j, n] = natural[band][place[KT_DEV * j + n]]
+        send_each(back_copy, band, me, ranks, start)
         landed[band][me] = slots[band][me]
 
     first_copies(wait_send)
@@ -372,12 +409,12 @@
     for step in range(1, pairs):
         panel_copy(step).wait_send()
     for band in (0, 1):
-        each(plane, lambda step: out_copy(band, step).wait_send())
+        send_each(out_copy, band, spot_in_plane, plane, wait_send)
 
     for band in (0, 1):
         low, high = bands[band]
         part = (high - low) // plane
-        each(ranks, lambda step: back_copy(band, step).wait_recv())
+        take_each(back_copy, band, me, ranks)
         for j in range(ranks):
             at = ((j % 4) // 2) * half + low + ((j // 4) * 2 + j % 2) * part
             for n in range(KT_DEV):
@@ -386,7 +423,7 @@
                     landed[band][j, n].astype(jnp.float32) + base[at : at + part, columns]
                 ).astype(out.dtype)
     for band in (0, 1):
-        each(ranks, lambda step: back_copy(band, step).wait_send())
+        send_each(back_copy, band, me, ranks, wait_send)
 
 
 def local(ranks, pairs, amplitudes, tile_owner, integrals, screening, occ_energy, virt_energy):
@@ -399,15 +436,16 @@
     dma = pltpu.SemaphoreType.DMA
     sizes = [(high - low) // plane for low, high in band_edges(half)]
 
-    def exchange(lead, tiles_each):
-        return [pltpu.VMEM((lead, tiles_each, size, TILE), jnp.bfloat16) for size in sizes]
+    def exchange(lead):
+        return [pltpu.VMEM((*lead, size, TILE), jnp.bfloat16) for size in sizes]
 
     return pl.pallas_call(
         functools.partial(ladder_kernel, ranks, pairs),
-        out_shape=jax.ShapeDtypeStruct((rows, width), jnp.bfloat16),
+        out_shape=pltpu.VMEM((rows, width), jnp.bfloat16),
         in_specs=[hbm] * 6,
         out_specs=pl.BlockSpec(memory_space=pltpu.VMEM),
         scratch_shapes=[
+            pltpu.SMEM((count,), jnp.int32),
             pltpu.SMEM((count,), jnp.int32),
             pltpu.SMEM((blocks, count, count), jnp.int32),
             pltpu.VMEM((rows // TILE, TILE), jnp.float32),
@@ -420,10 +458,10 @@
             pltpu.VMEM((KT_DEV * ranks, TILE, width), jnp.bfloat16),
             pltpu.VMEM((KT_DEV, half, width), jnp.bfloat16),
             pltpu.VMEM((half, 2 * width), jnp.float32),
-            *exchange(plane, 2 * KT_DEV),
-            *exchange(plane, 2 * KT_DEV),
-            *exchange(ranks, KT_DEV),
-            *exchange(ranks, KT_DEV),
+            *exchange((plane, 2 * KT_DEV)),
+            *exchange((plane * 2 * KT_DEV,)),
+            *exchange((ranks, KT_DEV)),
+            *exchange((ranks, KT_DEV)),
             dma((7,)),
             dma((2, 4, ranks)),
             dma((2, ranks)),
@@ -433,10 +471,10 @@
             dma((ranks,)),
             dma((pairs - 1, KT_DEV * ranks)),
             dma((KT_DEV * ranks,)),
-            dma((2, plane - 1)),
-            dma((2, plane - 1)),
-            dma((2, ranks - 1)),
-            dma((2, ranks - 1)),
+            dma((2, plane)),
+            dma((2, plane)),
+            dma((2, ranks)),
+            dma((2, ranks)),
         ],
         compiler_params=pltpu.CompilerParams(
             collective_id=0, has_side_effects=True, vmem_limit_bytes=62 * 1024 * 1024

time: 59.8 us -> 56.5 us (0.945)
  Pallas kernels: 57.9 us -> 55.6 us
  local copies, waits for them, and re-layouts: 1.72 us -> 0.73 us
    pallas_call x1, Pallas kernels: 57.9 us -> 55.6 us  [local(): pl.pallas_call(functools.partial(ladder_kernel, ranks, pairs), out_shape=...]
    unnamed x1, local copies, waits for them, and re-layouts: 1.72 us -> 0.73 us
where the time goes in v3:
time: 56.5 us; the launch traced here: 56.3 us
  Pallas kernels  55.6 us (98%)
  local copies, waits for them, and re-layouts  0.73 us (1%)
    pallas_call x1, Pallas kernels, local(): pl.pallas_call(functools.partial(ladder_kernel, ranks, pairs), out_shape=...  55.6 us

profile of v3, /device:TPU:0, one launch (start us, length us, event | category | flops | bytes accessed | tf_op | source)
XLA Modules:
  0.0 56.3 jit_solution(6842445223348234609)
XLA Ops:
  0.0 55.6 %shard_map.64 = bf16[640,256]{1,0:T(8,128)(2,1)S(1)} custom-call(bf16[640,256]{1,0:T(8,128)(2,1)} %amps.1, s32[32]{0:T(128)} %owner_in.1, bf16[16,128,256]{2,1,0:T(8,128)(2,1)} %bitcast.3, s32[10,32,32]{2,1,0:T(8,128)} %screen_in.1, f32[5,128]{1,0:T(8,128)} %bitcast.5, f32[32,128]{1,0:T(8,128)} %bitcast.4), custom_call_target="tpu_custom_call" | custom-call | tf_op jit(solution)/shard_map/pallas_call | solution.py:442
  55.6 0.7 %copy.8 = bf16[640,256]{1,0:T(8,128)(2,1)} copy(bf16[640,256]{1,0:T(8,128)(2,1)S(1)} %shard_map.64) | data formatting | bytes 655360

commit v4 on v3

--- a/solution.py
+++ b/solution.py
@@ -12,17 +12,20 @@
 KT_DEV = 2
 MESH = pl.DeviceIdType.MESH
 UP, DOWN, BESIDE, PARTNER = 0, 1, 2, 3
+SHARES = (2,)
+BANDS = range(len(SHARES) + 1)
 
 
 def band_edges(half):
-    cut = (half // PBLK * 3 // 5) * PBLK
-    return ((0, cut), (cut, half))
+    blocks = half // PBLK
+    edges = [0, *(blocks * share // 5 * PBLK for share in SHARES), half]
+    return tuple(zip(edges[:-1], edges[1:]))
 
 
 def ladder_kernel(
     ranks, pairs, amps, owner_in, ints, screen_in, occ_in, virt_in, out,
     owner, place, screen, occ, virt, mine, base, gath, panel, stage, far, lhs, acc,
-    parts0, parts1, natural0, natural1, slots0, slots1, landed0, landed1,
+    parts, natural, slots, landed,
     local_sem, send_sem, recv_sem, pair_send, pair_recv, far_send, far_recv, pass_send, pass_recv,
     out_send, out_recv, back_send, back_recv,
 ):
@@ -165,7 +168,7 @@
             pl.when(wanted & (mate < line))(lambda: action(relay(source, band, DOWN, me - 4)))
 
     def first_copies(action):
-        for band in (0, 1):
+        for band in BANDS:
             action(first_copy(band, PARTNER, partner))
             pl.when(has_up)(lambda: action(first_copy(band, UP, me + 4)))
             pl.when(has_down)(lambda: action(first_copy(band, DOWN, me - 4)))
@@ -265,7 +268,7 @@
         return lambda x, at, h, odd: action(unit(at, h, x))
 
     def relay_level(level):
-        for band in (0, 1):
+        for band in BANDS:
 
             def take(x, at, h, odd):
                 arrived(unit(at, h, x), band)
@@ -276,11 +279,16 @@
     def near_level(level):
         on_level(level, on_unit(lambda source: multiply(source, 0, 0, blocks)))
 
+    final = 2 * length + 1
+    skipped_unit = unit(skip, 1 - hi, 1)
+    outer = (line == 0) | (line == length - 1)
+    lag = jnp.where(outer, 1, 2)
+
     def early_level(level, _):
         relay_level(level)
-        on_level(level - 1, on_unit(pass_on))
+        on_level(level - lag, on_unit(pass_on))
         near_level(level)
-        on_level(level - 1, on_unit(far_whole))
+        on_level(level - lag, on_unit(far_whole))
         return 0
 
     def late_level(level, _):
@@ -290,76 +298,120 @@
         on_level(level - 1, on_unit(far_whole))
         return 0
 
-    final = 2 * length + 1
-    skipped_unit = unit(skip, 1 - hi, 1)
-
     lax.fori_loop(1, final - 2, early_level, 0)
-    on_level(final - 3, on_unit(pass_on))
-    lax.fori_loop(final - 2, final, late_level, 0)
-    on_level(final, on_unit(pass_on))
-    pass_on(skipped_unit)
-    on_level(final - 1, on_unit(far_whole))
-    on_level(final, on_unit(passed))
-    passed(skipped_unit)
 
     spot_in_plane = line * 2 + lo
-    parts, natural = (parts0, parts1), (natural0, natural1)
-    slots, landed = (slots0, slots1), (landed0, landed1)
-
-    def nearest(k, here, count):
-        wide = count // length
-        d = k // wide
-        low = jnp.minimum(line, length - 1 - line)
-        paired = line + ((d + 1) // 2) * (1 - 2 * (d % 2))
-        single = jnp.where(line < length // 2, d, length - 1 - d)
-        return jnp.where(d <= 2 * low, paired, single) * wide + (here + k) % wide
-
-    def out_copy(band, source, target):
+
+    flips = [1 - 2 * lo, 2 * (1 - 2 * hi)]
+    for bit in range(length.bit_length() - 1):
+        flips.append((4 << bit) * (1 - 2 * ((line // (1 << bit)) % 2)))
+
+    def moved(mask):
+        return sum(flip for bit, flip in enumerate(flips) if mask >> bit & 1)
+
+    def whole(buffer, count, send, recv):
+        place = buffer.at[pl.ds(0, count)]
         return pltpu.make_async_remote_copy(
-            src_ref=parts[band].at[target], dst_ref=natural[band].at[pl.ds(source * 4, 4)],
-            send_sem=out_send.at[band, target], recv_sem=out_recv.at[band, source],
-            device_id={"vcol": (target // 2) * 4 + hi * 2 + target % 2}, device_id_type=MESH,
-        )
-
-    def back_copy(band, source, target):
-        return pltpu.make_async_remote_copy(
-            src_ref=slots[band].at[target], dst_ref=landed[band].at[source],
-            send_sem=back_send.at[band, target], recv_sem=back_recv.at[band, source],
-            device_id={"vcol": target}, device_id_type=MESH,
-        )
-
-    def send_each(copy, band, here, count, action):
-        def body(step, _):
-            action(copy(band, here, nearest(count - step, here, count)))
-            return 0
-
-        lax.fori_loop(1, count, body, 0)
-
-    def take_each(copy, band, here, count):
-        def body(step, _):
-            copy(band, (here + step) % count, here).wait_recv()
-            return 0
-
-        lax.fori_loop(1, count, body, 0)
-
-    for band in (0, 1):
+            src_ref=place, dst_ref=place, send_sem=send, recv_sem=recv,
+            device_id={"vcol": beside}, device_id_type=MESH,
+        )
+
+    def send_slots(band):
+        for mask in reversed(range(1, ranks)):
+            target = me + moved(mask)
+            pltpu.make_async_remote_copy(
+                src_ref=slots[band].at[target], dst_ref=landed[band].at[me],
+                send_sem=back_send.at[band], recv_sem=back_recv.at[band],
+                device_id={"vcol": target}, device_id_type=MESH,
+            ).start()
+
+    def send_parts(side, band):
+        for mask in reversed(range(1, ranks)):
+            if mask & 2 == 0:
+                target = me + moved(mask)
+                column = spot_in_plane + moved(mask & 1) + moved(mask & -4) // 2
+                pltpu.make_async_remote_copy(
+                    src_ref=parts[band].at[side, column],
+                    dst_ref=natural[band].at[
+                        pl.ds((spot_in_plane * 2 + side) * KT_DEV, KT_DEV)
+                    ],
+                    send_sem=out_send.at[side, band], recv_sem=out_recv.at[band],
+                    device_id={"vcol": target}, device_id_type=MESH,
+                ).start()
+
+    def parts_taken(band):
+        return whole(
+            natural[band], (plane - 1) * 2 * KT_DEV, out_send.at[0, band], out_recv.at[band]
+        )
+
+    def parts_sent(side, band):
+        return whole(
+            parts[band].at[side], plane - 1, out_send.at[side, band], out_recv.at[band]
+        )
+
+    def slots_moved(band):
+        return whole(slots[band], ranks - 1, back_send.at[band], back_recv.at[band])
+
+    def send_out(side, band):
         low, high = bands[band]
-
-        def finish(source):
-            arrived(source, band)
-            for side in (0, 1):
-                multiply(source, side, low // PBLK, high // PBLK)
-
-        on_level(final, on_unit(finish))
-        finish(skipped_unit)
         part = (high - low) // plane
         for i in range(plane):
-            for n in range(2 * KT_DEV):
-                parts[band][i, n] = acc[
-                    low + i * part : low + (i + 1) * part, n * TILE : (n + 1) * TILE
+            for n in range(KT_DEV):
+                column = (side * KT_DEV + n) * TILE
+                parts[band][side, i, n] = acc[
+                    low + i * part : low + (i + 1) * part, column : column + TILE
                 ].astype(jnp.bfloat16)
-        send_each(out_copy, band, spot_in_plane, plane, start)
-        natural[band][pl.ds(spot_in_plane * 4, 4)] = parts[band][spot_in_plane]
+        send_parts(side, band)
+        natural[band][pl.ds((spot_in_plane * 2 + side) * KT_DEV, KT_DEV)] = parts[band][
+            side, spot_in_plane
+        ]
+
+    @pl.when(outer)
+    def _():
+        on_level(final - 3, on_unit(pass_on))
+        lax.fori_loop(final - 2, final, late_level, 0)
+        on_level(final, on_unit(pass_on))
+        pass_on(skipped_unit)
+        on_level(final - 1, on_unit(far_whole))
+        on_level(final, on_unit(passed))
+        passed(skipped_unit)
+        for band in BANDS:
+            low, high = bands[band]
+
+            def finish(source):
+                arrived(source, band)
+                for side in (0, 1):
+                    multiply(source, side, low // PBLK, high // PBLK)
+
+            on_level(final, on_unit(finish))
+            finish(skipped_unit)
+            for side in (0, 1):
+                send_out(side, band)
+
+    @pl.when(~outer)
+    def _():
+        relay_level(final - 2)
+        near_level(final - 2)
+        for band in BANDS:
+            arrived(skipped_unit, band)
+        multiply(skipped_unit, 0, 0, blocks)
+        for band in BANDS:
+            send_out(0, band)
+
+        def rest(level, _):
+            on_level(level, on_unit(pass_on))
+            on_level(level - 1, on_unit(far_whole))
+            return 0
+
+        on_level(final - 4, on_unit(pass_on))
+        lax.fori_loop(final - 3, final - 1, rest, 0)
+        pass_on(skipped_unit)
+        on_level(final - 2, on_unit(far_whole))
+        passed(skipped_unit)
+        for band in BANDS:
+            low, high = bands[band]
+            multiply(skipped_unit, 1, low // PBLK, high // PBLK)
+            send_out(1, band)
 
     get_occ.wait()
     get_virt.wait()
@@ -377,18 +429,18 @@
             level = virt[pl.ds(owner[KT_DEV * me + n], 1), :]
             base[part, columns] = (level - column) * mine[part, columns].astype(jnp.float32)
 
-    for band in (0, 1):
-        take_each(out_copy, band, spot_in_plane, plane)
+    for band in BANDS:
+        parts_taken(band).wait_recv()
         for j in range(ranks):
             for n in range(KT_DEV):
                 slots[band][j, n] = natural[band][place[KT_DEV * j + n]]
-        send_each(back_copy, band, me, ranks, start)
+        send_slots(band)
         landed[band][me] = slots[band][me]
 
     first_copies(wait_send)
 
     def drain(level, _):
-        for band in (0, 1):
+        for band in BANDS:
             on_level(
                 level, lambda x, at, h, odd: onward(x, at, h, odd, band, wait_send)
             )
@@ -408,13 +460,14 @@
     lax.fori_loop(0, ranks, close, 0)
     for step in range(1, pairs):
         panel_copy(step).wait_send()
-    for band in (0, 1):
-        send_each(out_copy, band, spot_in_plane, plane, wait_send)
-
-    for band in (0, 1):
+    for band in BANDS:
+        for side in (0, 1):
+            parts_sent(side, band).wait_send()
+
+    for band in BANDS:
         low, high = bands[band]
         part = (high - low) // plane
-        take_each(back_copy, band, me, ranks)
+        slots_moved(band).wait_recv()
         for j in range(ranks):
             at = ((j % 4) // 2) * half + low + ((j // 4) * 2 + j % 2) * part
             for n in range(KT_DEV):
@@ -422,8 +475,8 @@
                 out[at : at + part, columns] = (
                     landed[band][j, n].astype(jnp.float32) + base[at : at + part, columns]
                 ).astype(out.dtype)
-    for band in (0, 1):
-        send_each(back_copy, band, me, ranks, wait_send)
+    for band in BANDS:
+        slots_moved(band).wait_send()
 
 
 def local(ranks, pairs, amplitudes, tile_owner, integrals, screening, occ_energy, virt_energy):
@@ -458,23 +511,23 @@
             pltpu.VMEM((KT_DEV * ranks, TILE, width), jnp.bfloat16),
             pltpu.VMEM((KT_DEV, half, width), jnp.bfloat16),
             pltpu.VMEM((half, 2 * width), jnp.float32),
-            *exchange((plane, 2 * KT_DEV)),
-            *exchange((plane * 2 * KT_DEV,)),
-            *exchange((ranks, KT_DEV)),
-            *exchange((ranks, KT_DEV)),
+            exchange((2, plane, KT_DEV)),
+            exchange((plane * 2 * KT_DEV,)),
+            exchange((ranks, KT_DEV)),
+            exchange((ranks, KT_DEV)),
             dma((7,)),
-            dma((2, 4, ranks)),
-            dma((2, ranks)),
+            dma((len(BANDS), 4, ranks)),
+            dma((len(BANDS), ranks)),
             dma((pairs - 1,)),
             dma((pairs - 1,)),
             dma((ranks,)),
             dma((ranks,)),
             dma((pairs - 1, KT_DEV * ranks)),
             dma((KT_DEV * ranks,)),
-            dma((2, plane)),
-            dma((2, plane)),
-            dma((2, ranks)),
-            dma((2, ranks)),
+            dma((2, len(BANDS))),
+            dma((len(BANDS),)),
+            dma((len(BANDS),)),
+            dma((len(BANDS),)),
         ],
         compiler_params=pltpu.CompilerParams(
             collective_id=0, has_side_effects=True, vmem_limit_bytes=62 * 1024 * 1024

time: 56.5 us -> 53.5 us (0.947)
  Pallas kernels: 55.6 us -> 52.6 us
    pallas_call x1, Pallas kernels: 55.6 us -> 52.6 us  [local(): pl.pallas_call(functools.partial(ladder_kernel, ranks, pairs), out_shape=...]
where the time goes in v4:
time: 53.5 us; the launch traced here: 53.3 us
  Pallas kernels  52.6 us (98%)
  local copies, waits for them, and re-layouts  0.73 us (1%)
    pallas_call x1, Pallas kernels, local(): pl.pallas_call(functools.partial(ladder_kernel, ranks, pairs), out_shape=...  52.6 us

profile of v4, /device:TPU:0, one launch (start us, length us, event | category | flops | bytes accessed | tf_op | source)
XLA Modules:
  0.0 53.3 jit_solution(15582663568894498095)
XLA Ops:
  0.0 52.6 %shard_map.64 = bf16[640,256]{1,0:T(8,128)(2,1)S(1)} custom-call(bf16[640,256]{1,0:T(8,128)(2,1)} %amps.1, s32[32]{0:T(128)} %owner_in.1, bf16[16,128,256]{2,1,0:T(8,128)(2,1)} %bitcast.3, s32[10,32,32]{2,1,0:T(8,128)} %screen_in.1, f32[5,128]{1,0:T(8,128)} %bitcast.5, f32[32,128]{1,0:T(8,128)} %bitcast.4), custom_call_target="tpu_custom_call" | custom-call | tf_op jit(solution)/shard_map/pallas_call | solution.py:495
  52.6 0.7 %copy.8 = bf16[640,256]{1,0:T(8,128)(2,1)} copy(bf16[640,256]{1,0:T(8,128)(2,1)S(1)} %shard_map.64) | data formatting | bytes 655360

commit v5 on v4

--- a/solution.py
+++ b/solution.py
@@ -12,13 +12,13 @@
 KT_DEV = 2
 MESH = pl.DeviceIdType.MESH
 UP, DOWN, BESIDE, PARTNER = 0, 1, 2, 3
-SHARES = (2,)
-BANDS = range(len(SHARES) + 1)
-
-
-def band_edges(half):
+SHARES, LEGS = (2,), (2,)
+BANDS, HAULS = range(len(SHARES) + 1), range(len(LEGS) + 1)
+
+
+def band_edges(half, shares):
     blocks = half // PBLK
-    edges = [0, *(blocks * share // 5 * PBLK for share in SHARES), half]
+    edges = [0, *(blocks * share // 5 * PBLK for share in shares), half]
     return tuple(zip(edges[:-1], edges[1:]))
 
 
@@ -42,7 +42,7 @@
     half = gath.shape[1]
     blocks = half // PBLK
     tiles = ints.shape[0]
-    bands = band_edges(half)
+    bands, hauls = band_edges(half, SHARES), band_edges(half, LEGS)
 
     def load(index, source, target):
         return pltpu.make_async_copy(source, target, local_sem.at[index])
@@ -76,7 +76,7 @@
     )
 
     def first_copy(band, way, target):
-        low, high = bands[band]
+        low, high = hauls[band]
         start_row = (1 - hi) * half if way == PARTNER else hi * half
         return pltpu.make_async_remote_copy(
             src_ref=amps.at[pl.ds(start_row + low, high - low)],
@@ -86,7 +86,7 @@
         )
 
     def relay(source, band, way, target):
-        low, high = bands[band]
+        low, high = hauls[band]
         place = gath.at[source, pl.ds(low, high - low)]
         return pltpu.make_async_remote_copy(
             src_ref=place, dst_ref=place,
@@ -168,7 +168,7 @@
             pl.when(wanted & (mate < line))(lambda: action(relay(source, band, DOWN, me - 4)))
 
     def first_copies(action):
-        for band in BANDS:
+        for band in HAULS:
             action(first_copy(band, PARTNER, partner))
             pl.when(has_up)(lambda: action(first_copy(band, UP, me + 4)))
             pl.when(has_down)(lambda: action(first_copy(band, DOWN, me - 4)))
@@ -215,7 +215,7 @@
         )
         return 0
 
-    def to_partner(action):
+    def to_partner(action, first, stop):
         def body(level, _):
             def send(x, at, h, odd):
                 source = unit(at, 1 - h, x)
@@ -224,12 +224,14 @@
             on_level(level, send)
             return 0
 
-        lax.fori_loop(0, 2 * length + 2, body, 0)
+        lax.fori_loop(first, stop, body, 0)
+
+    def skipped_to_partner(action):
         source = unit(skip, hi, 1)
         if_holder(source, core, lambda: action(far_copy(source)))
 
     lax.fori_loop(0, ranks, fill, 0)
-    to_partner(start)
+    to_partner(start, 0, 3)
 
     def pass_on(source):
         def go():
@@ -253,22 +255,11 @@
         passed(source)
         multiply(source, 1, 0, blocks)
 
-    def find(slot, _):
-        tile = owner[slot]
-        row, col = (tile >> 2) & 1, (tile >> 1) & 1
-        place[slot] = (tile & -8) | (col << 2) | ((row ^ hi) << 1) | (tile & 1)
-        return 0
-
-    lax.fori_loop(0, KT_DEV * ranks, find, 0)
-    get_screen.wait()
-    own_amps.wait()
-    multiply(me, 0, 0, blocks)
-
     def on_unit(action):
         return lambda x, at, h, odd: action(unit(at, h, x))
 
     def relay_level(level):
-        for band in BANDS:
+        for band in HAULS:
 
             def take(x, at, h, odd):
                 arrived(unit(at, h, x), band)
@@ -285,7 +276,7 @@
     lag = jnp.where(outer, 1, 2)
 
     def early_level(level, _):
-        relay_level(level)
+        pl.when(level > 1)(lambda: relay_level(level))
         on_level(level - lag, on_unit(pass_on))
         near_level(level)
         on_level(level - lag, on_unit(far_whole))
@@ -298,6 +289,12 @@
         on_level(level - 1, on_unit(far_whole))
         return 0
 
+    relay_level(1)
+    to_partner(start, 3, 2 * length + 2)
+    skipped_to_partner(start)
+    get_screen.wait()
+    own_amps.wait()
+    multiply(me, 0, 0, blocks)
     lax.fori_loop(1, final - 2, early_level, 0)
 
     spot_in_plane = line * 2 + lo
@@ -379,20 +376,25 @@
             low, high = bands[band]
 
             def finish(source):
-                arrived(source, band)
-                for side in (0, 1):
-                    multiply(source, side, low // PBLK, high // PBLK)
+                for haul, (top, _) in enumerate(hauls):
+                    if low <= top < high:
+                        arrived(source, haul)
 
             on_level(final, on_unit(finish))
             finish(skipped_unit)
             for side in (0, 1):
+                part = functools.partial(
+                    multiply, side=side, first=low // PBLK, stop=high // PBLK
+                )
+                on_level(final, on_unit(part))
+                part(skipped_unit)
                 send_out(side, band)
 
     @pl.when(~outer)
     def _():
         relay_level(final - 2)
         near_level(final - 2)
-        for band in BANDS:
+        for band in HAULS:
             arrived(skipped_unit, band)
         multiply(skipped_unit, 0, 0, blocks)
         for band in BANDS:
@@ -413,6 +415,13 @@
             multiply(skipped_unit, 1, low // PBLK, high // PBLK)
             send_out(1, band)
 
+    def find(slot, _):
+        tile = owner[slot]
+        row, col = (tile >> 2) & 1, (tile >> 1) & 1
+        place[slot] = (tile & -8) | (col << 2) | ((row ^ hi) << 1) | (tile & 1)
+        return 0
+
+    lax.fori_loop(0, KT_DEV * ranks, find, 0)
     get_occ.wait()
     get_virt.wait()
     get_mine.wait()
@@ -440,14 +449,15 @@
     first_copies(wait_send)
 
     def drain(level, _):
-        for band in BANDS:
+        for band in HAULS:
             on_level(
                 level, lambda x, at, h, odd: onward(x, at, h, odd, band, wait_send)
             )
         return 0
 
     lax.fori_loop(1, final + 1, drain, 0)
-    to_partner(wait_send)
+    to_partner(wait_send, 0, 2 * length + 2)
+    skipped_to_partner(wait_send)
 
     def close(source, _):
         def go():
@@ -487,7 +497,7 @@
     blocks = half // PBLK
     hbm = pl.BlockSpec(memory_space=pl.ANY)
     dma = pltpu.SemaphoreType.DMA
-    sizes = [(high - low) // plane for low, high in band_edges(half)]
+    sizes = [(high - low) // plane for low, high in band_edges(half, SHARES)]
 
     def exchange(lead):
         return [pltpu.VMEM((*lead, size, TILE), jnp.bfloat16) for size in sizes]
@@ -516,8 +526,8 @@
             exchange((ranks, KT_DEV)),
             exchange((ranks, KT_DEV)),
             dma((7,)),
-            dma((len(BANDS), 4, ranks)),
-            dma((len(BANDS), ranks)),
+            dma((len(HAULS), 4, ranks)),
+            dma((len(HAULS), ranks)),
             dma((pairs - 1,)),
             dma((pairs - 1,)),
             dma((ranks,)),

time: 53.5 us -> 53.1 us (level)
  no operation moved by 1% of the time
where the time goes in v5:
time: 53.1 us; the launch traced here: 53 us
  Pallas kernels  52.2 us (98%)
  local copies, waits for them, and re-layouts  0.73 us (1%)
    pallas_call x1, Pallas kernels, local(): pl.pallas_call(functools.partial(ladder_kernel, ranks, pairs), out_shape=...  52.2 us

profile of v5, /device:TPU:0, one launch (start us, length us, event | category | flops | bytes accessed | tf_op | source)
XLA Modules:
  0.0 53.0 jit_solution(17064788928132068460)
XLA Ops:
  0.0 52.2 %shard_map.64 = bf16[640,256]{1,0:T(8,128)(2,1)S(1)} custom-call(bf16[640,256]{1,0:T(8,128)(2,1)} %amps.1, s32[32]{0:T(128)} %owner_in.1, bf16[16,128,256]{2,1,0:T(8,128)(2,1)} %bitcast.3, s32[10,32,32]{2,1,0:T(8,128)} %screen_in.1, f32[5,128]{1,0:T(8,128)} %bitcast.5, f32[32,128]{1,0:T(8,128)} %bitcast.4), custom_call_target="tpu_custom_call" | custom-call | tf_op jit(solution)/shard_map/pallas_call | solution.py:505
  52.2 0.7 %copy.8 = bf16[640,256]{1,0:T(8,128)(2,1)} copy(bf16[640,256]{1,0:T(8,128)(2,1)S(1)} %shard_map.64) | data formatting | bytes 655360

commit v6 on v5

--- a/solution.py
+++ b/solution.py
@@ -279,7 +279,7 @@
         pl.when(level > 1)(lambda: relay_level(level))
         on_level(level - lag, on_unit(pass_on))
         near_level(level)
-        on_level(level - lag, on_unit(far_whole))
+        on_level(level - lag - 1, on_unit(far_whole))
         return 0
 
     def late_level(level, _):
@@ -366,6 +366,7 @@
     @pl.when(outer)
     def _():
         on_level(final - 3, on_unit(pass_on))
+        on_level(final - 4, on_unit(far_whole))
         lax.fori_loop(final - 2, final, late_level, 0)
         on_level(final, on_unit(pass_on))
         pass_on(skipped_unit)
@@ -406,6 +407,7 @@
             return 0
 
         on_level(final - 4, on_unit(pass_on))
+        on_level(final - 5, on_unit(far_whole))
         lax.fori_loop(final - 3, final - 1, rest, 0)
         pass_on(skipped_unit)
         on_level(final - 2, on_unit(far_whole))

time: 53.1 us -> 53 us (level)
  no operation moved by 1% of the time
where the time goes in v6:
time: 53 us; the launch traced here: 52.9 us
  Pallas kernels  52.2 us (98%)
  local copies, waits for them, and re-layouts  0.73 us (1%)
    pallas_call x1, Pallas kernels, local(): pl.pallas_call(functools.partial(ladder_kernel, ranks, pairs), out_shape=...  52.2 us

profile of v6, /device:TPU:0, one launch (start us, length us, event | category | flops | bytes accessed | tf_op | source)
XLA Modules:
  0.0 52.9 jit_solution(7517820512300611715)
XLA Ops:
  0.0 52.2 %shard_map.64 = bf16[640,256]{1,0:T(8,128)(2,1)S(1)} custom-call(bf16[640,256]{1,0:T(8,128)(2,1)} %amps.1, s32[32]{0:T(128)} %owner_in.1, bf16[16,128,256]{2,1,0:T(8,128)(2,1)} %bitcast.3, s32[10,32,32]{2,1,0:T(8,128)} %screen_in.1, f32[5,128]{1,0:T(8,128)} %bitcast.5, f32[32,128]{1,0:T(8,128)} %bitcast.4), custom_call_target="tpu_custom_call" | custom-call | tf_op jit(solution)/shard_map/pallas_call | solution.py:507
  52.2 0.7 %copy.8 = bf16[640,256]{1,0:T(8,128)(2,1)} copy(bf16[640,256]{1,0:T(8,128)(2,1)S(1)} %shard_map.64) | data formatting | bytes 655360
